TPU v7x, 32 devices: a whole 2x2x4 slice. The times are simulated.
32 devices in a mesh: dp: 8 (over y, x, core), tensor: 4 (over z).
Axes of the slice: x: 2, y: 2, z: 4, core: 2. Of those that a mesh axis runs over, the one named last changes fastest.
Arguments:
- clip_rows: bfloat16 [12544, 1024], P(('dp', 'tensor')), may hold values from -6 to 6
- out_grad: bfloat16 [12544, 1024], P(('dp', 'tensor')), may hold values from -6 to 6
- clip_valid: int32 [8], P('dp'), may hold values from 0 to 1, as said below
- gain_rows: bfloat16 [2, 1024], P(None, ('dp', 'tensor')), may hold values from 0.099609375 to 1.8984375
- bias_rows: bfloat16 [4, 1024], P(None, ('dp', 'tensor')), may hold values from -1.796875 to 1.796875
- qkv_weight: bfloat16 [3, 1024, 1024], P(None, 'dp', 'tensor'), may hold values from -0.1875 to 0.1875
- qv_bias: bfloat16 [2, 16, 64], P(None, 'tensor', 'dp'), may hold values from -3 to 3
- proj_weight: bfloat16 [1024, 1024], P('tensor', 'dp'), may hold values from -4 to 4
- fc1_weight: bfloat16 [1024, 4096], P('dp', 'tensor'), may hold values from -0.1875 to 0.1875
- fc1_bias: bfloat16 [4, 1024], P('tensor', 'dp'), may hold values from -1.796875 to 1.796875
- fc2_weight: bfloat16 [4096, 1024], P('tensor', 'dp'), may hold values from -0.125 to 0.125
Outputs:
- layer_out: bfloat16 [12544, 1024], P(('dp', 'tensor'))
- input_grad: float32 [12544, 1024], P(('dp', 'tensor'))
- grad_gains: float32 [2, 1024], P(None, ('dp', 'tensor'))
- grad_biases: float32 [4, 1024], P(None, ('dp', 'tensor'))
- grad_qkv: float32 [3, 1024, 1024], P(None, 'dp', 'tensor')
- grad_qv_bias: float32 [2, 16, 64], P(None, 'tensor', 'dp')
- grad_proj: float32 [1024, 1024], P('tensor', 'dp')
- grad_fc1: float32 [1024, 4096], P('dp', 'tensor')
- grad_fc1_bias: float32 [4, 1024], P('tensor', 'dp')
- grad_fc2: float32 [4096, 1024], P('tensor', 'dp')
- grad_fc2_bias: float32 [1024], P(('dp', 'tensor'))
Inputs may be any that keep to these rules, and one draw needn't show every extreme that they name: `clip_valid`: exactly 2 of the 8 slots hold a clip; which ones is drawn from the seed.
All inputs are finite; a program needn't handle non-finite values.
Results may differ from a plain program's by a relative error of at most 0.012.
Values may be sent and summed in bfloat16 or wider, within the bound.
No kernel may reach another device: no remote copies, remote signals or barrier semaphores. Data moves between devices by JAX's collectives and lax.ppermute only.
A program may use at most 256 MiB of HBM per device.

v0:
```python
import math
import jax
import jax.numpy as jnp
from jax import lax
from jax.sharding import PartitionSpec as P

HD = 64
norm_eps = 1e-06
root_half = 0.7071067811865476
inv_root_tau = 0.3989422804014327


def normalize(values, gain_row, shift_row):
    centre = jnp.mean(values, axis=1, keepdims=True)
    offsets = values - centre
    inverse = lax.rsqrt(jnp.mean(offsets * offsets, axis=1, keepdims=True) + norm_eps)
    scaled = offsets * inverse
    return (scaled * gain_row + shift_row, scaled, inverse)


def normalize_back(upstream, scaled, inverse, gain_row):
    grad_hat = upstream * gain_row
    return (
        grad_hat
        - jnp.mean(grad_hat, axis=1, keepdims=True)
        - scaled * jnp.mean(grad_hat * scaled, axis=1, keepdims=True)
    ) * inverse


def gelu_value(inputs):
    return 0.5 * inputs * (1.0 + lax.erf(inputs * root_half))


def gelu_slope(inputs):
    return (
        0.5 * (1.0 + lax.erf(inputs * root_half))
        + inputs * jnp.exp(-0.5 * inputs * inputs) * inv_root_tau
    )


def fetch(qkv_weight, proj_weight, fc1_weight, fc2_weight, qv_bias, fc1_bias, gain_rows, bias_rows):
    matrices = (
        lax.all_gather(qkv_weight, "dp", axis=1, tiled=True),
        lax.all_gather(proj_weight, "dp", axis=1, tiled=True),
        lax.all_gather(fc1_weight, "dp", axis=0, tiled=True),
        lax.all_gather(fc2_weight, "dp", axis=1, tiled=True),
        lax.all_gather(qv_bias, "dp", axis=2, tiled=True),
        lax.all_gather(fc1_bias, "dp", axis=1, tiled=True),
    )
    vectors = (
        lax.all_gather(gain_rows, ("dp", "tensor"), axis=1, tiled=True),
        lax.all_gather(bias_rows, ("dp", "tensor"), axis=1, tiled=True),
    )
    return (matrices, (vectors[0].astype(jnp.float32), vectors[1].astype(jnp.float32)))


def spread_rows(local_rows):
    return lax.all_gather(local_rows, "tensor", axis=0, tiled=True)


def reduce_rows(term_fn, row_count):
    return lax.psum_scatter(
        term_fn(jnp.int32(0), lax.axis_size("tensor") * row_count),
        "tensor",
        scatter_dimension=0,
        tiled=True,
    )


def spread_grads(local_rows):
    return lax.all_gather(local_rows, "tensor", axis=0, tiled=True)


def reduce_grads(term_fn, row_count):
    return lax.psum_scatter(
        term_fn(jnp.int32(0), lax.axis_size("tensor") * row_count),
        "tensor",
        scatter_dimension=0,
        tiled=True,
    )


def forward(clip_rows, matrices, vectors):
    w_qkv, w_proj, w_fc1, w_fc2, b_qv, b_fc1 = matrices
    gain_rows, bias_rows = vectors
    row_count = clip_rows.shape[0]
    head_cols = w_qkv.shape[2]
    heads_here = head_cols // HD
    score_scale = 1.0 / math.sqrt(HD)
    inputs = clip_rows.astype(jnp.float32)
    normed_one, scaled_one, inverse_one = normalize(inputs, gain_rows[0], bias_rows[0])
    whole_one = spread_rows(normed_one.astype(jnp.bfloat16))
    seq_len = whole_one.shape[0]
    projected = jnp.einsum("sd,jde->jse", whole_one, w_qkv, preferred_element_type=jnp.float32)
    bias_cols = b_qv.reshape(2, head_cols).astype(jnp.float32)
    queries = (projected[0] + bias_cols[0]).astype(jnp.bfloat16).reshape(seq_len, heads_here, HD)
    keys_all = projected[1].astype(jnp.bfloat16).reshape(seq_len, heads_here, HD)
    values_all = (projected[2] + bias_cols[1]).astype(jnp.bfloat16).reshape(seq_len, heads_here, HD)
    scores = (
        jnp.einsum("qhd,khd->hqk", queries, keys_all, preferred_element_type=jnp.float32)
        * score_scale
    )
    top_score = jnp.max(scores, axis=2, keepdims=True)
    weights_exp = jnp.exp(scores - top_score)
    totals = jnp.sum(weights_exp, axis=2, keepdims=True)
    attn_probs = (weights_exp / totals).astype(jnp.bfloat16)
    log_total = top_score + jnp.log(totals)
    attended = (
        jnp.einsum("hqk,khd->qhd", attn_probs, values_all, preferred_element_type=jnp.float32)
        .reshape(seq_len, head_cols)
        .astype(jnp.bfloat16)
    )

    def proj_term(offset, length):
        return jnp.dot(attended, w_proj, preferred_element_type=jnp.float32)

    residual_one = inputs + (reduce_rows(proj_term, row_count) + bias_rows[2])
    normed_two, scaled_two, inverse_two = normalize(residual_one, gain_rows[1], bias_rows[1])
    whole_two = spread_rows(normed_two.astype(jnp.bfloat16))
    pre_act = jnp.dot(whole_two, w_fc1, preferred_element_type=jnp.float32) + b_fc1.reshape(
        -1
    ).astype(jnp.float32)
    hidden = gelu_value(pre_act).astype(jnp.bfloat16)

    def fc2_term(offset, length):
        return jnp.dot(hidden, w_fc2, preferred_element_type=jnp.float32)

    layer_out = residual_one + (reduce_rows(fc2_term, row_count) + bias_rows[3])
    stored = (
        scaled_one,
        inverse_one,
        whole_one,
        queries,
        keys_all,
        values_all,
        log_total,
        attended,
        scaled_two,
        inverse_two,
        whole_two,
        pre_act,
        hidden,
    )
    return (layer_out, stored)


def backward(upstream, matrices, vectors, stored):
    w_qkv, w_proj, w_fc1, w_fc2, b_qv, b_fc1 = matrices
    gain_rows, bias_rows = vectors
    (
        scaled_one,
        inverse_one,
        whole_one,
        queries,
        keys_all,
        values_all,
        log_total,
        attended,
        scaled_two,
        inverse_two,
        whole_two,
        pre_act,
        hidden,
    ) = stored
    row_count = upstream.shape[0]
    seq_len = queries.shape[0]
    heads_here = queries.shape[1]
    head_cols = heads_here * HD
    score_scale = 1.0 / math.sqrt(HD)
    grad_mlp = upstream.astype(jnp.bfloat16)
    grad_fc2_bias = jnp.sum(grad_mlp.astype(jnp.float32), axis=0)
    whole_mlp = spread_grads(grad_mlp)
    grad_fc2 = jnp.einsum("sf,sd->fd", hidden, whole_mlp, preferred_element_type=jnp.float32)
    grad_hidden = jnp.einsum("sd,fd->sf", whole_mlp, w_fc2, preferred_element_type=jnp.float32)
    grad_pre = (grad_hidden * gelu_slope(pre_act)).astype(jnp.bfloat16)
    grad_fc1_bias = jnp.sum(grad_pre.astype(jnp.float32), axis=0)
    grad_fc1 = jnp.einsum("sd,sf->df", whole_two, grad_pre, preferred_element_type=jnp.float32)

    def fc1_back(offset, length):
        return jnp.einsum("sf,df->sd", grad_pre, w_fc1, preferred_element_type=jnp.float32)

    grad_normed_two = reduce_grads(fc1_back, row_count)
    grad_residual = upstream + normalize_back(
        grad_normed_two, scaled_two, inverse_two, gain_rows[1]
    )
    grad_branch = grad_residual.astype(jnp.bfloat16)
    grad_proj_bias = jnp.sum(grad_branch.astype(jnp.float32), axis=0)
    whole_branch = spread_grads(grad_branch)
    grad_proj = jnp.einsum("se,sd->ed", attended, whole_branch, preferred_element_type=jnp.float32)
    grad_att = (
        jnp.einsum("sd,ed->se", whole_branch, w_proj, preferred_element_type=jnp.float32)
        .astype(jnp.bfloat16)
        .reshape(seq_len, heads_here, HD)
    )
    scores = (
        jnp.einsum("qhd,khd->hqk", queries, keys_all, preferred_element_type=jnp.float32)
        * score_scale
    )
    attn_probs = jnp.exp(scores - log_total)
    grad_probs = jnp.einsum(
        "qhd,khd->hqk", grad_att, values_all, preferred_element_type=jnp.float32
    )
    row_dot = jnp.sum(attn_probs * grad_probs, axis=2, keepdims=True)
    grad_scores = (attn_probs * (grad_probs - row_dot)).astype(jnp.bfloat16)
    grad_query = (
        jnp.einsum("hqk,khd->qhd", grad_scores, keys_all, preferred_element_type=jnp.float32)
        * score_scale
    ).astype(jnp.bfloat16)
    grad_key = (
        jnp.einsum("hqk,qhd->khd", grad_scores, queries, preferred_element_type=jnp.float32)
        * score_scale
    ).astype(jnp.bfloat16)
    grad_value = jnp.einsum(
        "hqk,qhd->khd",
        attn_probs.astype(jnp.bfloat16),
        grad_att,
        preferred_element_type=jnp.float32,
    ).astype(jnp.bfloat16)
    grad_qkv = jnp.stack([grad_query, grad_key, grad_value]).reshape(3, seq_len, head_cols)
    grad_qv = jnp.stack(
        [
            jnp.sum(grad_query.astype(jnp.float32), axis=0),
            jnp.sum(grad_value.astype(jnp.float32), axis=0),
        ]
    )
    grad_qkv_weight = jnp.einsum(
        "sd,jse->jde", whole_one, grad_qkv, preferred_element_type=jnp.float32
    )

    def qkv_back(offset, length):
        return jnp.einsum("jse,jde->sd", grad_qkv, w_qkv, preferred_element_type=jnp.float32)

    grad_normed_one = reduce_grads(qkv_back, row_count)
    grad_input = grad_residual + normalize_back(
        grad_normed_one, scaled_one, inverse_one, gain_rows[0]
    )
    grad_gain = jnp.stack(
        [
            jnp.sum(grad_normed_one * scaled_one, axis=0),
            jnp.sum(grad_normed_two * scaled_two, axis=0),
        ]
    )
    grad_bias = jnp.stack(
        [
            jnp.sum(grad_normed_one, axis=0),
            jnp.sum(grad_normed_two, axis=0),
            grad_proj_bias,
            grad_fc2_bias,
        ]
    )
    weight_part = (
        lax.psum_scatter(grad_qkv_weight, "dp", scatter_dimension=1, tiled=True),
        lax.psum_scatter(grad_proj, "dp", scatter_dimension=1, tiled=True),
        lax.psum_scatter(grad_fc1, "dp", scatter_dimension=0, tiled=True),
        lax.psum_scatter(grad_fc2, "dp", scatter_dimension=1, tiled=True),
        lax.psum_scatter(grad_qv, "dp", scatter_dimension=2, tiled=True),
        lax.psum_scatter(grad_fc1_bias.reshape(1, -1), "dp", scatter_dimension=1, tiled=True),
    )
    vector_part = (
        lax.psum_scatter(grad_gain, ("dp", "tensor"), scatter_dimension=1, tiled=True),
        lax.psum_scatter(grad_bias, ("dp", "tensor"), scatter_dimension=1, tiled=True),
    )
    return (grad_input, weight_part, vector_part)


def on_device(
    clip_rows,
    out_grad,
    clip_valid,
    gain_rows,
    bias_rows,
    qkv_weight,
    qv_bias,
    proj_weight,
    fc1_weight,
    fc1_bias,
    fc2_weight,
):
    clip_weight = clip_valid[0].astype(jnp.float32)
    upstream = out_grad.astype(jnp.float32) * clip_weight
    matrices, vectors = fetch(
        qkv_weight, proj_weight, fc1_weight, fc2_weight, qv_bias, fc1_bias, gain_rows, bias_rows
    )
    layer_out, stored = forward(clip_rows, matrices, vectors)
    matrices, vectors = fetch(
        qkv_weight, proj_weight, fc1_weight, fc2_weight, qv_bias, fc1_bias, gain_rows, bias_rows
    )
    unused_out, stored = forward(clip_rows, matrices, vectors)
    grad_input, weight_part, vector_part = backward(upstream, matrices, vectors, stored)
    return (
        (layer_out * clip_weight).astype(jnp.bfloat16),
        grad_input,
        vector_part[0],
        vector_part[1],
        weight_part[0],
        weight_part[4],
        weight_part[1],
        weight_part[2],
        weight_part[5],
        weight_part[3],
        vector_part[1][3],
    )


def solution(mesh):
    in_specs = (
        P(("dp", "tensor"), None),
        P(("dp", "tensor"), None),
        P("dp"),
        P(None, ("dp", "tensor")),
        P(None, ("dp", "tensor")),
        P(None, "dp", "tensor"),
        P(None, "tensor", "dp"),
        P("tensor", "dp"),
        P("dp", "tensor"),
        P("tensor", "dp"),
        P("tensor", "dp"),
    )
    out_specs = (
        P(("dp", "tensor"), None),
        P(("dp", "tensor"), None),
        P(None, ("dp", "tensor")),
        P(None, ("dp", "tensor")),
        P(None, "dp", "tensor"),
        P(None, "tensor", "dp"),
        P("tensor", "dp"),
        P("dp", "tensor"),
        P("tensor", "dp"),
        P("tensor", "dp"),
        P(("dp", "tensor")),
    )
    return jax.shard_map(
        on_device, mesh=mesh, in_specs=in_specs, out_specs=out_specs, check_vma=False
    )
```

profile of v0, /device:TPU:0, one launch (start us, length us, event | category | flops | bytes accessed | tf_op | source)
XLA Modules:
  0.0 1630.0 jit_solution(12553502785783311040)
XLA Ops:
  8.0 69.5 %all-gather = bf16[32,32,2]{1,2,0:T(2,128)(2,1)S(1)} all-gather(bf16[1,32,2]{1,2,0:T(2,128)(2,1)} %bitcast.144), channel_id=1, replica_groups=mesh['dp'=8,'tensor'=4] {'dp','tensor'}, dimensions={0}, use_global_device_ids=true | all-gather | bytes 4224 | tf_op jit(solution)/shard_map/all_gather | solution.py:51
  77.5 63.8 %all-gather.1 = bf16[32,32,4]{1,2,0:T(4,128)(2,1)S(1)} all-gather(bf16[1,32,4]{1,2,0:T(4,128)(2,1)} %bitcast.143), channel_id=1, replica_groups=mesh['dp'=8,'tensor'=4] {'dp','tensor'}, dimensions={0}, use_global_device_ids=true | all-gather | bytes 8448 | tf_op jit(solution)/shard_map/all_gather | solution.py:52
  141.4 1.4 convert_reduce_fusion.1
  142.8 1.5 fusion.37
  144.9 1.2 fusion.31
  146.4 8.1 all_gather.50
  154.6 11.0 all_gather.51
  165.6 43.3 %all-gather.10.cloned.1.call-done = bf16[1568,1024]{1,0:T(8,128)(2,1)} async-done(((bf16[392,1024]{1,0:T(8,128)(2,1)}), bf16[1568,1024]{1,0:T(8,128)(2,1)}) %all-gather.10.cloned.1.call-update) | async-done | bytes 3211280 | tf_op jit(solution)/shard_map/all_gather | solution.py:58
  208.9 5.1 convolution_bitcast_fusion.1
  215.0 1.4 fusion.44
  216.3 1.5 copy.74
  217.9 1.7 copy.69
  219.5 1.8 copy.72
  221.3 16.1 fusion.48
  237.5 16.4 %fusion = f32[4,1568]{1,0:T(4,128)S(1)} fusion(f32[4,1568,1568]{1,2,0:T(8,128)} %get-tuple-element.82, f32[4,1568]{1,0:T(4,128)S(1)} %get-tuple-element.81), kind=kLoop, calls=%fused_computation.6 | loop fusion | flops 19662720 | bytes 39388160 | tf_op jit(solution)/shard_map/reduce_sum | solution.py:105
  253.8 17.4 %fusion.20 = bf16[4,64,1568]{2,1,0:T(8,128)(2,1)} fusion(f32[4,1568,1568]{1,2,0:T(8,128)} %get-tuple-element.82, f32[4,1568]{1,0:T(4,128)S(1)} %fusion, f32[4,1568]{1,0:T(4,128)S(1)} %get-tuple-element.81, f32[1568,4,64]{0,2,1:T(8,128)S(1)} %bitcast.106, f32[4,64]{1,0:T(4,128)S(1)} %copy.71), kind=kOutput, calls=%fused_computation.32 | convolution fusion | flops 1289523200 | bytes 41797632 | tf_op jit(solution)/shard_map/hqk,khd->qhd/dot_general | solution.py:109
  271.3 4.9 fusion.49
  277.2 110.7 %reduce-scatter.19.cloned.1.call-done = f32[392,1024]{1,0:T(8,128)} async-done(((f32[1568,1024]{1,0:T(8,128)}), f32[392,1024]{1,0:T(8,128)}) %reduce-scatter.19.cloned.1.call-update) | async-done | bytes 1605648 | tf_op jit(solution)/shard_map/reduce_scatter | solution.py:62
  387.9 1.7 fusion.43
  389.9 1.2 add_convert_fusion.2
  392.5 1.1 convert_reduce_fusion.4
  393.6 8.7 all_gather.54
  402.4 15.7 all-gather.16.cloned.1.call-done
  418.1 66.6 %all-gather.14.cloned.1.call-done = bf16[1568,1024]{1,0:T(8,128)(2,1)} async-done(((bf16[392,1024]{1,0:T(8,128)(2,1)}), bf16[1568,1024]{1,0:T(8,128)(2,1)}) %all-gather.14.cloned.1.call-update) | async-done | bytes 3211280 | tf_op jit(solution)/shard_map/all_gather | solution.py:58
  484.7 8.5 multiply_convert_fusion.1
  493.2 20.1 %all-gather.18.cloned.1.call-done = bf16[1024,1024]{1,0:T(8,128)(2,1)} async-done(((bf16[1024,128]{1,0:T(8,128)(2,1)}), bf16[1024,1024]{1,0:T(8,128)(2,1)}) %all-gather.18.cloned.1.call-update) | async-done | bytes 2097168 | tf_op jit(solution)/shard_map/all_gather | solution.py:46
  513.3 66.8 %all-gather.20.cloned.1.call-done = bf16[1568,1024]{1,0:T(8,128)(2,1)} async-done(((bf16[392,1024]{1,0:T(8,128)(2,1)}), bf16[1568,1024]{1,0:T(8,128)(2,1)}) %all-gather.20.cloned.1.call-update) | async-done | bytes 3211280 | tf_op jit(solution)/shard_map/all_gather | solution.py:71
  580.0 9.5 convert_reduce_fusion
  589.6 1.7 copy-done.30
  591.3 5.7 fusion.51
  597.0 8.8 fusion.50
  605.9 102.8 %reduce-scatter.23.cloned.1.call-done = f32[392,1024]{1,0:T(8,128)} async-done(((f32[1568,1024]{1,0:T(8,128)}), f32[392,1024]{1,0:T(8,128)}) %reduce-scatter.23.cloned.1.call-update) | async-done | bytes 1605648 | tf_op jit(solution)/shard_map/reduce_scatter | solution.py:75
  708.6 2.1 multiply_reduce_fusion.1
  710.8 113.6 %reduce-scatter.21.cloned.1.call-done = f32[392,1024]{1,0:T(8,128)} async-done(((f32[1568,1024]{1,0:T(8,128)}), f32[392,1024]{1,0:T(8,128)}) %reduce-scatter.21.cloned.1.call-update) | async-done | bytes 1605648 | tf_op jit(solution)/shard_map/reduce_scatter | solution.py:62
  824.4 4.4 convert_reduce_fusion.5
  828.9 65.2 %all-gather.22.cloned.1.call-done = bf16[1568,1024]{1,0:T(8,128)(2,1)} async-done(((bf16[392,1024]{1,0:T(8,128)(2,1)}), bf16[1568,1024]{1,0:T(8,128)(2,1)}) %all-gather.22.cloned.1.call-update) | async-done | bytes 3211280 | tf_op jit(solution)/shard_map/all_gather | solution.py:71
  894.1 3.0 convolution_convert_fusion
  898.0 16.9 %convert_reduce_fusion.2 = (f32[4,64]{1,0:T(4,128)S(1)}, bf16[4,64,1568]{2,1,0:T(8,128)(2,1)}) fusion(bf16[1568,4,64]{0,2,1:T(8,128)(2,1)S(1)} %bitcast.104, f32[4,1568,1568]{1,2,0:T(8,128)} %get-tuple-element.82, f32[4,1568]{1,0:T(4,128)S(1)} %log_add_fusion), kind=kOutput, calls=%fused_computation.44 | convolution fusion | flops 1279688448 | bytes 40969728 | tf_op jit(solution)/shard_map/hqk,qhd->khd/dot_general | solution.py:213
  914.9 26.3 %multiply_reduce_fusion = (f32[4,1568]{1,0:T(4,128)S(1)}, f32[4,1568,1568]{1,2,0:T(8,128)}) fusion(f32[4,1568,1568]{1,2,0:T(8,128)} %get-tuple-element.82, f32[4,1568]{1,0:T(4,128)S(1)} %log_add_fusion, bf16[1568,4,64]{0,2,1:T(8,128)(2,1)S(1)} %bitcast.105, f32[1568,4,64]{0,2,1:T(8,128)S(1)} %bitcast.107, f32[4,64]{1,0:T(4,128)S(1)} %copy.71), kind=kOutput, calls=%fused_computation.1 | convolution fusion | flops 1289115520 | bytes 81135616 | tf_op jit(solution)/shard_map/qhd,khd->hqk/dot_general | solution.py:200
  941.2 33.6 %multiply_convert_fusion = bf16[4,1568,1568]{1,2,0:T(8,128)(2,1)} fusion(f32[4,1568,1568]{1,2,0:T(8,128)} %get-tuple-element.86, f32[4,1568,1568]{1,2,0:T(8,128)} %get-tuple-element.82, f32[4,1568]{1,0:T(4,128)S(1)} %get-tuple-element.85, f32[4,1568]{1,0:T(4,128)S(1)} %log_add_fusion), kind=kLoop, calls=%fused_computation | loop fusion | flops 39337984 | bytes 98395136 | tf_op jit(solution)/shard_map/convert_element_type | solution.py:204
  974.8 11.4 fusion.16
  986.2 10.4 convert_reduce_fusion.3
  996.7 1.2 copy.82
  997.9 1.2 copy.80
  999.9 7.3 convolution_bitcast_fusion
  1008.8 6.7 fusion.27
  1015.6 103.3 %reduce-scatter.25.cloned.1.call-done = f32[392,1024]{1,0:T(8,128)} async-done(((f32[1568,1024]{1,0:T(8,128)}), f32[392,1024]{1,0:T(8,128)}) %reduce-scatter.25.cloned.1.call-update) | async-done | bytes 1605648 | tf_op jit(solution)/shard_map/reduce_scatter | solution.py:75
  1119.0 2.2 fusion.36
  1123.4 8.8 fusion.53
  1132.6 8.9 fusion.54
  1141.6 1.1 copy-done.11
  1142.7 4.0 fusion.52
  1148.0 8.6 reduce-scatter.39.cloned.1.call-done
  1156.6 1.4 copy.95
  1158.0 12.2 all-reduce
  1170.9 35.7 %reduce-scatter.27.cloned.1.call-done = f32[3,128,256]{1,2,0:T(8,128)} async-done(((f32[3,1024,256]{1,2,0:T(8,128)}), f32[3,128,256]{1,2,0:T(8,128)}) %reduce-scatter.27.cloned.1.call-update) | async-done | bytes 393232 | tf_op jit(solution)/shard_map/reduce_scatter | solution.py:252
  1206.6 1.9 copy.83
  1208.5 3.1 fusion.35
  1211.7 131.5 %reduce-scatter.35.cloned.1.call-done = f32[32,2]{1,0:T(8,128)} async-done(((f32[1024,2]{1,0:T(8,128)}), f32[32,2]{1,0:T(8,128)}) %reduce-scatter.35.cloned.1.call-update) | async-done | bytes 272
  1343.2 1.4 copy.89
  1344.6 131.6 %reduce-scatter.37.cloned.1.call-done = f32[32,4]{1,0:T(8,128)} async-done(((f32[1024,4]{1,0:T(8,128)}), f32[32,4]{1,0:T(8,128)}) %reduce-scatter.37.cloned.1.call-update) | async-done | bytes 528
  1477.5 50.1 %reduce-scatter.31.cloned.1.call-done = f32[128,1024]{1,0:T(8,128)} async-done(((f32[1024,1024]{1,0:T(8,128)}), f32[128,1024]{1,0:T(8,128)}) %reduce-scatter.31.cloned.1.call-update) | async-done | bytes 524304 | tf_op jit(solution)/shard_map/reduce_scatter | solution.py:254
  1527.6 55.5 %reduce-scatter.33.cloned.1.call-done = f32[1024,128]{1,0:T(8,128)} async-done(((f32[1024,1024]{1,0:T(8,128)}), f32[1024,128]{1,0:T(8,128)}) %reduce-scatter.33.cloned.1.call-update) | async-done | bytes 524304 | tf_op jit(solution)/shard_map/reduce_scatter | solution.py:255
  1583.1 39.6 %reduce-scatter.29.cloned.1.call-done = f32[256,128]{1,0:T(8,128)} async-done(((f32[256,1024]{1,0:T(8,128)}), f32[256,128]{1,0:T(8,128)}) %reduce-scatter.29.cloned.1.call-update) | async-done | bytes 131088 | tf_op jit(solution)/shard_map/reduce_scatter | solution.py:253
  (130 shorter events, 13.5 us)
Async XLA Ops:
  7.2 137.8 %copy-start.2 = (bf16[392,1024]{1,0:T(8,128)(2,1)S(1)}, bf16[392,1024]{1,0:T(8,128)(2,1)}, u32[]{:S(2)}) copy-start(bf16[392,1024]{1,0:T(8,128)(2,1)} %param.11) | copy-start | bytes 2408452
  7.2 158.4 %all-gather.12.cloned.1.call-start = ((), (), s32[]{:S(2)}) async-start(), calls=%async_computation.12 | async-start | bytes 1769472 | tf_op jit(solution)/shard_map/all_gather | solution.py:43
  7.9 201.0 %all-gather.10.cloned.1.call-start = ((), (), s32[]{:S(2)}) async-start(), calls=%async_computation.11 | async-start | bytes 4014080 | tf_op jit(solution)/shard_map/all_gather | solution.py:58
  141.3 4.9 copy-start.25
  141.4 13.2 copy-start.20
  142.8 71.2 %copy-start.21 = (f32[392]{0:T(512)}, f32[392]{0:T(512)S(1)}, u32[]{:S(2)}) copy-start(f32[392]{0:T(512)S(1)} %broadcast_multiply_fusion.5) | copy-start | bytes 4708
  144.3 69.7 %copy-start.23 = (f32[392]{0:T(512)}, f32[392]{0:T(512)S(1)}, u32[]{:S(2)}) copy-start(f32[392]{0:T(512)S(1)} %add_rsqrt_fusion.1) | copy-start | bytes 4708
  144.3 0.6 copy-start.18
  146.2 241.7 %reduce-scatter.19.cloned.1.call-start = ((), (), s32[]{:S(2)}) async-start(), calls=%async_computation.13 | async-start | bytes 8028160 | tf_op jit(solution)/shard_map/reduce_scatter | solution.py:62
  154.6 66.7 %copy-start.16 = (f32[4,64]{1,0:T(4,128)}, f32[4,64]{1,0:T(4,128)S(1)}, u32[]{:S(2)}) copy-start(f32[4,64]{1,0:T(4,128)S(1)} %copy.73) | copy-start | bytes 3076
  217.9 3.4 copy-start
  221.3 16.2 copy-start.3
  237.4 16.4 %copy-start.5 = (f32[1,1568,256]{1,2,0:T(8,128)S(1)}, f32[1,1568,256]{1,2,0:T(8,128)}, u32[]{:S(2)}) copy-start(f32[1,1568,256]{1,2,0:T(8,128)} %copy.69) | copy-start | bytes 4816900
  253.8 17.4 %copy-start.10 = (bf16[256,1024]{1,0:T(8,128)(2,1)S(1)}, bf16[256,1024]{1,0:T(8,128)(2,1)}, u32[]{:S(2)}) copy-start(bf16[256,1024]{1,0:T(8,128)(2,1)} %all_gather.51) | copy-start | bytes 1572868
  276.2 141.9 %all-gather.16.cloned.1.call-start = ((), (), s32[]{:S(2)}) async-start(), calls=%async_computation.15 | async-start | bytes 2359296 | tf_op jit(solution)/shard_map/all_gather | solution.py:45
  276.8 207.9 %all-gather.14.cloned.1.call-start = ((), (), s32[]{:S(2)}) async-start(), calls=%async_computation.14 | async-start | bytes 4014080 | tf_op jit(solution)/shard_map/all_gather | solution.py:58
  389.9 2.5 copy-start.9
  391.2 2.5 copy-start.27
  391.2 122.1 %all-gather.18.cloned.1.call-start = ((), (), s32[]{:S(2)}) async-start(), calls=%async_computation.16 | async-start | bytes 2359296 | tf_op jit(solution)/shard_map/all_gather | solution.py:46
  391.8 188.3 %all-gather.20.cloned.1.call-start = ((), (), s32[]{:S(2)}) async-start(), calls=%async_computation.18 | async-start | bytes 4014080 | tf_op jit(solution)/shard_map/all_gather | solution.py:71
  393.6 315.1 %reduce-scatter.23.cloned.1.call-start = ((), (), s32[]{:S(2)}) async-start(), calls=%async_computation.19 | async-start | bytes 8028160 | tf_op jit(solution)/shard_map/reduce_scatter | solution.py:75
  580.0 11.2 copy-start.28
  589.6 1.7 copy-start.30
  597.0 227.4 %reduce-scatter.21.cloned.1.call-start = ((), (), s32[]{:S(2)}) async-start(), calls=%async_computation.17 | async-start | bytes 8028160 | tf_op jit(solution)/shard_map/reduce_scatter | solution.py:62
  605.8 288.3 %all-gather.22.cloned.1.call-start = ((), (), s32[]{:S(2)}) async-start(), calls=%async_computation.20 | async-start | bytes 4014080 | tf_op jit(solution)/shard_map/all_gather | solution.py:71
  828.8 290.1 %reduce-scatter.25.cloned.1.call-start = ((), (), s32[]{:S(2)}) async-start(), calls=%async_computation.21 | async-start | bytes 8028160 | tf_op jit(solution)/shard_map/reduce_scatter | solution.py:75
  898.0 16.9 %copy-start.6 = (f32[1,1568,256]{1,2,0:T(8,128)S(1)}, f32[1,1568,256]{1,2,0:T(8,128)}, u32[]{:S(2)}) copy-start(f32[1,1568,256]{1,2,0:T(8,128)} %copy.69) | copy-start | bytes 4816900
  941.2 33.6 %copy-start.4 = (f32[1,1568,256]{1,2,0:T(8,128)S(1)}, f32[1,1568,256]{1,2,0:T(8,128)}, u32[]{:S(2)}) copy-start(f32[1,1568,256]{1,2,0:T(8,128)} %copy-done.3) | copy-start | bytes 4816900
  941.2 33.6 %copy-start.17 = (f32[4,64]{1,0:T(4,128)S(1)}, f32[4,64]{1,0:T(4,128)}, u32[]{:S(2)}) copy-start(f32[4,64]{1,0:T(4,128)} %copy-done.16) | copy-start | bytes 3076
  974.8 11.4 copy-start.1
  986.2 10.4 copy-start.8
  997.9 2.0 copy-start.12
  999.9 7.3 copy-start.14
  1007.2 1.2 copy-start.13
  1007.3 1.6 copy-start.15
  1007.3 149.3 %reduce-scatter.39.cloned.1.call-start = ((), (), s32[]{:S(2)}) async-start(), calls=%async_computation.28 | async-start | bytes 589824
  1008.4 198.2 %reduce-scatter.27.cloned.1.call-start = ((), (), s32[]{:S(2)}) async-start(), calls=%async_computation.22 | async-start | bytes 3538944 | tf_op jit(solution)/shard_map/reduce_scatter | solution.py:252
  1015.5 103.4 %copy-start.19 = (f32[1,1024]{1,0:T(1,128)S(1)}, f32[1,1024]{1,0:T(1,128)}, u32[]{:S(2)}) copy-start(f32[1,1024]{1,0:T(1,128)} %copy-done.18) | copy-start | bytes 12292
  1015.5 103.4 %copy-start.22 = (f32[392]{0:T(512)S(1)}, f32[392]{0:T(512)}, u32[]{:S(2)}) copy-start(f32[392]{0:T(512)} %copy-done.21) | copy-start | bytes 4708
  1015.5 103.4 %copy-start.24 = (f32[392]{0:T(512)S(1)}, f32[392]{0:T(512)}, u32[]{:S(2)}) copy-start(f32[392]{0:T(512)} %copy-done.23) | copy-start | bytes 4708
  1015.6 327.6 %reduce-scatter.35.cloned.1.call-start = ((), (), s32[]{:S(2)}) async-start(), calls=%async_computation.26 | async-start | bytes 540672
  1122.2 353.9 %reduce-scatter.37.cloned.1.call-start = ((), (), s32[]{:S(2)}) async-start(), calls=%async_computation.27 | async-start | bytes 540672
  1123.4 404.2 %reduce-scatter.31.cloned.1.call-start = ((), (), s32[]{:S(2)}) async-start(), calls=%async_computation.24 | async-start | bytes 4718592 | tf_op jit(solution)/shard_map/reduce_scatter | solution.py:254
  1132.3 450.8 %reduce-scatter.33.cloned.1.call-start = ((), (), s32[]{:S(2)}) async-start(), calls=%async_computation.25 | async-start | bytes 4718592 | tf_op jit(solution)/shard_map/reduce_scatter | solution.py:255
  1141.5 1.2 copy-start.11
  1141.5 5.2 copy-start.29
  1141.5 481.2 %reduce-scatter.29.cloned.1.call-start = ((), (), s32[]{:S(2)}) async-start(), calls=%async_computation.23 | async-start | bytes 1179648 | tf_op jit(solution)/shard_map/reduce_scatter | solution.py:253
  1146.7 61.8 %copy-start.7 = (f32[392,1024]{1,0:T(8,128)S(1)}, f32[392,1024]{1,0:T(8,128)}, u32[]{:S(2)}) copy-start(f32[392,1024]{1,0:T(8,128)} %reduce-scatter.25.cloned.1.call-done) | copy-start | bytes 4816900
  1476.9 145.8 %copy-start.26 = (f32[4,32]{1,0:T(4,128)}, f32[4,32]{1,0:T(4,128)S(1)}, u32[]{:S(2)}) copy-start(f32[4,32]{1,0:T(4,128)S(1)} %copy.91) | copy-start | bytes 1540
Sparse Core Ops, SparseCore 0:
  9.9 28.3 all-gather.11
  146.3 62.5 all-gather.9
  276.3 111.5 reduce-scatter.18
  389.6 28.3 all-gather.15
  420.1 64.5 all-gather.13
  486.4 26.8 all-gather.17
  515.4 64.5 all-gather.19
  597.1 111.5 reduce-scatter.22
  711.0 113.3 reduce-scatter.20
  829.0 65.0 all-gather.21
  1007.4 111.5 reduce-scatter.24
  1121.9 34.6 reduce-scatter.38
  1160.3 46.2 reduce-scatter.26
  1208.7 134.4 reduce-scatter.34
  1345.4 130.7 reduce-scatter.36
  1479.9 47.6 reduce-scatter.30
  1531.7 51.3 reduce-scatter.32
  1586.7 35.9 reduce-scatter.28
where the time goes:
time: 1640 us; the launch traced here: 1630 us
  waiting for transfers between devices  1160 us (71%)
  matrix products  180 us (11%)
  blocking collectives  173 us (11%)
  other arithmetic  70.3 us (4%)
  local copies, waits for them, and re-layouts  26 us (2%)
  between operations  16.5 us (1%)
    unnamed x21, waiting for transfers between devices  274 us
    reduce_scatter x2, waiting for transfers between devices, reduce_rows(): lax.psum_scatter(term_fn(jnp.int32(0), lax.axis_size('tensor') * row_coun...  224 us
    reduce_scatter x2, waiting for transfers between devices, reduce_grads(): lax.psum_scatter(term_fn(jnp.int32(0), lax.axis_size('tensor') * row_coun...  206 us
    all_gather x2, waiting for transfers between devices, spread_grads(): return lax.all_gather(local_rows, 'tensor', axis=0, tiled=True)  132 us
    all_gather x2, waiting for transfers between devices, spread_rows(): return lax.all_gather(local_rows, 'tensor', axis=0, tiled=True)  110 us
    all_gather x1, blocking collectives, fetch(): lax.all_gather(gain_rows, ('dp', 'tensor'), axis=1, tiled=True)  69.5 us
    all_gather x1, blocking collectives, fetch(): lax.all_gather(bias_rows, ('dp', 'tensor'), axis=1, tiled=True)  63.8 us
    reduce_scatter x1, waiting for transfers between devices, backward(): lax.psum_scatter(grad_fc2, 'dp', scatter_dimension=1, tiled=True)  55.5 us
  transfers between devices with their start and end apart: 18, of which 17 were waited for; matrix products, arithmetic and copies ran while one was open for 4% of the time, Pallas kernels for 0%

commit v1 on v0

--- a/solution.py
+++ b/solution.py
@@ -3,6 +3,7 @@
 import jax.numpy as jnp
 from jax import lax
 from jax.sharding import PartitionSpec as P
+from jax.lax import axis_index, axis_size, ppermute
 
 HD = 64
 norm_eps = 1e-06
@@ -55,7 +56,32 @@
 
 
 def spread_rows(local_rows):
-    return lax.all_gather(local_rows, "tensor", axis=0, tiled=True)
+
+    def _obtain_loads(chunk, a_name):
+        latest = axis_size(a_name)
+        even = axis_index(a_name)
+        local_next, y2, met_up = (latest, even, chunk.shape[0])
+        tray = tuple(((idx, (idx + 1) % local_next) for idx in range(local_next)))
+        made = tuple(((idx, (idx - 1) % local_next) for idx in range(local_next)))
+        piece_next = jnp.zeros(
+            (*chunk.shape[:0], local_next * met_up, *chunk.shape[1:]), chunk.dtype
+        )
+        piece_next = lax.dynamic_update_slice_in_dim(piece_next, chunk, y2 * met_up, axis=0)
+        far_arr = moved = chunk
+        z1 = local_next // 2
+        for i in tuple(range(1, z1 + 1)):
+            far_arr = ppermute(far_arr, a_name, tray)
+            piece_next = lax.dynamic_update_slice_in_dim(
+                piece_next, far_arr, (y2 - i) % local_next * met_up, axis=0
+            )
+            if i < local_next - z1:
+                moved = ppermute(moved, a_name, made)
+                piece_next = lax.dynamic_update_slice_in_dim(
+                    piece_next, moved, (y2 + i) % local_next * met_up, axis=0
+                )
+        return piece_next
+
+    return _obtain_loads(local_rows, "tensor")
 
 
 def reduce_rows(term_fn, row_count):

time: 1640 us -> 1560 us (0.951)
  waiting for transfers between devices: 1160 us -> 1050 us
  starting transfers between devices: 1.33 us -> 33.2 us
    all_gather x2 -> x0, waiting for transfers between devices: 110 us -> none  [spread_rows(): return lax.all_gather(local_rows, 'tensor', axis=0, tiled=True)]
    ppermute x0 -> x6, waiting for transfers between devices: none -> 45.6 us  [the longest x4 45.6 us: _obtain_loads(): far_arr = ppermute(far_arr, a_name, tray)]
    ppermute x0 -> x6, starting transfers between devices: none -> 31.7 us  [the longest x4 27.8 us: _obtain_loads(): far_arr = ppermute(far_arr, a_name, tray)]
    all_gather x1, waiting for transfers between devices: 20.1 us -> 0.01 us  [fetch(): lax.all_gather(fc2_weight, 'dp', axis=1, tiled=True)]
    unnamed x21 -> x19, waiting for transfers between devices: 274 us -> 273 us
  transfers between devices with their start and end apart: 18 -> 22, of which waited for: 17 -> 16; matrix products, arithmetic and copies ran while one was open for 4% -> 5% of each run, Pallas kernels for 0% -> 0%
where the time goes in v1:
time: 1560 us
  waiting for transfers between devices  1050 us (67%)
  matrix products  180 us (12%)
  blocking collectives  173 us (11%)
  other arithmetic  70.3 us (5%)
  local copies, waits for them, and re-layouts  36.3 us (2%)
  starting transfers between devices  33.2 us (2%)
  between operations  15.9 us (1%)
    unnamed x19, waiting for transfers between devices  273 us
    reduce_scatter x2, waiting for transfers between devices, reduce_rows(): lax.psum_scatter(term_fn(jnp.int32(0), lax.axis_size('tensor') * row_coun...  223 us
    reduce_scatter x2, waiting for transfers between devices, reduce_grads(): lax.psum_scatter(term_fn(jnp.int32(0), lax.axis_size('tensor') * row_coun...  206 us
    all_gather x2, waiting for transfers between devices, spread_grads(): return lax.all_gather(local_rows, 'tensor', axis=0, tiled=True)  121 us
    all_gather x1, blocking collectives, fetch(): lax.all_gather(gain_rows, ('dp', 'tensor'), axis=1, tiled=True)  69.6 us
    all_gather x1, blocking collectives, fetch(): lax.all_gather(bias_rows, ('dp', 'tensor'), axis=1, tiled=True)  63.7 us
    reduce_scatter x1, waiting for transfers between devices, backward(): lax.psum_scatter(grad_fc2, 'dp', scatter_dimension=1, tiled=True)  55.5 us
    reduce_scatter x1, waiting for transfers between devices, backward(): lax.psum_scatter(grad_fc1, 'dp', scatter_dimension=0, tiled=True)  50.1 us
  transfers between devices with their start and end apart: 22, of which 16 were waited for; matrix products, arithmetic and copies ran while one was open for 5% of the time, Pallas kernels for 0%

profile of v1, /device:TPU:0, one launch (start us, length us, event | category | flops | bytes accessed | tf_op | source)
XLA Modules:
  0.0 1559.0 jit_solution(508841865736207487)
XLA Ops:
  9.3 69.6 %all-gather = bf16[32,32,2]{1,2,0:T(2,128)(2,1)S(1)} all-gather(bf16[1,32,2]{1,2,0:T(2,128)(2,1)} %bitcast.144), channel_id=1, replica_groups=mesh['dp'=8,'tensor'=4] {'dp','tensor'}, dimensions={0}, use_global_device_ids=true | all-gather | bytes 4224 | tf_op jit(solution)/shard_map/all_gather | solution.py:52
  78.9 63.7 %all-gather.1 = bf16[32,32,4]{1,2,0:T(4,128)(2,1)S(1)} all-gather(bf16[1,32,4]{1,2,0:T(4,128)(2,1)} %bitcast.143), channel_id=1, replica_groups=mesh['dp'=8,'tensor'=4] {'dp','tensor'}, dimensions={0}, use_global_device_ids=true | all-gather | bytes 8448 | tf_op jit(solution)/shard_map/all_gather | solution.py:53
  142.7 1.5 fusion.37
  144.5 2.1 broadcast.95.clone
  147.8 2.3 collective-permute-start
  150.0 1.6 collective-permute-start.1
  151.7 18.8 %collective-permute-done = bf16[392,1024]{1,0:T(8,128)(2,1)S(1)} collective-permute-done((bf16[392,1024]{1,0:T(8,128)(2,1)S(1)}, bf16[392,1024]{1,0:T(8,128)(2,1)S(1)}, u32[]{:S(2)}, u32[]{:S(2)}) %collective-permute-start) | collective-permute-done | bytes 802848 | tf_op jit(solution)/shard_map/ppermute | solution.py:73
  170.5 9.4 collective-permute-start.2
  180.0 8.1 all_gather.41
  188.2 11.2 all_gather.42
  201.3 2.1 constant_dynamic-update-slice_fusion.4
  203.4 5.1 convolution_bitcast_fusion.1
  209.4 1.4 fusion.45
  210.8 1.5 copy.74
  212.3 1.6 copy.69
  214.0 1.8 copy.72
  215.8 16.1 %fusion.49 = (f32[4,1568]{1,0:T(4,128)S(1)}, f32[4,1568,1568]{1,2,0:T(8,128)}) fusion(bf16[1568,4,64]{0,2,1:T(8,128)(2,1)S(1)} %bitcast.99, f32[1568,4,64]{0,2,1:T(8,128)S(1)} %bitcast.102, f32[4,64]{1,0:T(4,128)S(1)} %copy.73), kind=kOutput, calls=%fused_computation.102 | convolution fusion | flops 1279281024 | bytes 41772544 | tf_op jit(solution)/shard_map/qhd,khd->hqk/dot_general | solution.py:126
  231.9 16.4 %fusion = f32[4,1568]{1,0:T(4,128)S(1)} fusion(f32[4,1568,1568]{1,2,0:T(8,128)} %get-tuple-element.86, f32[4,1568]{1,0:T(4,128)S(1)} %get-tuple-element.85), kind=kLoop, calls=%fused_computation.6 | loop fusion | flops 19662720 | bytes 39388160 | tf_op jit(solution)/shard_map/reduce_sum | solution.py:131
  248.3 17.4 %fusion.20 = bf16[4,64,1568]{2,1,0:T(8,128)(2,1)} fusion(f32[4,1568,1568]{1,2,0:T(8,128)} %get-tuple-element.86, f32[4,1568]{1,0:T(4,128)S(1)} %fusion, f32[4,1568]{1,0:T(4,128)S(1)} %get-tuple-element.85, f32[1568,4,64]{0,2,1:T(8,128)S(1)} %bitcast.106, f32[4,64]{1,0:T(4,128)S(1)} %copy.71), kind=kOutput, calls=%fused_computation.32 | convolution fusion | flops 1289523200 | bytes 41797632 | tf_op jit(solution)/shard_map/hqk,khd->qhd/dot_general | solution.py:135
  265.7 4.9 fusion.50
  273.8 109.5 %reduce-scatter.19.cloned.1.call-done = f32[392,1024]{1,0:T(8,128)} async-done(((f32[1568,1024]{1,0:T(8,128)}), f32[392,1024]{1,0:T(8,128)}) %reduce-scatter.19.cloned.1.call-update) | async-done | bytes 1605648 | tf_op jit(solution)/shard_map/reduce_scatter | solution.py:88
  383.4 1.7 fusion.43
  385.4 2.1 broadcast.95
  388.7 1.5 collective-permute-start.3
  390.3 2.3 collective-permute-start.4
  392.6 18.8 %collective-permute-done.3 = bf16[392,1024]{1,0:T(8,128)(2,1)S(1)} collective-permute-done((bf16[392,1024]{1,0:T(8,128)(2,1)S(1)}, bf16[392,1024]{1,0:T(8,128)(2,1)S(1)}, u32[]{:S(2)}, u32[]{:S(2)}) %collective-permute-start.3) | collective-permute-done | bytes 802848 | tf_op jit(solution)/shard_map/ppermute | solution.py:73
  411.4 14.6 collective-permute-start.5
  426.0 8.7 all_gather.44
  436.7 8.0 collective-permute-done.5
  445.6 8.5 multiply_convert_fusion.1
  454.2 56.1 %all-gather.14.cloned.1.call-done = bf16[1568,1024]{1,0:T(8,128)(2,1)} async-done(((bf16[392,1024]{1,0:T(8,128)(2,1)}), bf16[1568,1024]{1,0:T(8,128)(2,1)}) %all-gather.14.cloned.1.call-update) | async-done | bytes 3211280 | tf_op jit(solution)/shard_map/all_gather | solution.py:97
  510.3 9.5 convert_reduce_fusion
  519.8 1.7 copy-done.30
  521.5 5.7 fusion.52
  527.3 8.8 fusion.51
  536.3 102.6 %reduce-scatter.23.cloned.1.call-done = f32[392,1024]{1,0:T(8,128)} async-done(((f32[1568,1024]{1,0:T(8,128)}), f32[392,1024]{1,0:T(8,128)}) %reduce-scatter.23.cloned.1.call-update) | async-done | bytes 1605648 | tf_op jit(solution)/shard_map/reduce_scatter | solution.py:101
  638.9 2.1 multiply_reduce_fusion.1
  641.0 113.6 %reduce-scatter.21.cloned.1.call-done = f32[392,1024]{1,0:T(8,128)} async-done(((f32[1568,1024]{1,0:T(8,128)}), f32[392,1024]{1,0:T(8,128)}) %reduce-scatter.21.cloned.1.call-update) | async-done | bytes 1605648 | tf_op jit(solution)/shard_map/reduce_scatter | solution.py:88
  754.6 4.4 convert_reduce_fusion.5
  759.1 65.2 %all-gather.16.cloned.1.call-done = bf16[1568,1024]{1,0:T(8,128)(2,1)} async-done(((bf16[392,1024]{1,0:T(8,128)(2,1)}), bf16[1568,1024]{1,0:T(8,128)(2,1)}) %all-gather.16.cloned.1.call-update) | async-done | bytes 3211280 | tf_op jit(solution)/shard_map/all_gather | solution.py:97
  824.3 3.0 convolution_convert_fusion
  828.1 16.9 %convert_reduce_fusion.2 = (f32[4,64]{1,0:T(4,128)S(1)}, bf16[4,64,1568]{2,1,0:T(8,128)(2,1)}) fusion(bf16[1568,4,64]{0,2,1:T(8,128)(2,1)S(1)} %bitcast.104, f32[4,1568,1568]{1,2,0:T(8,128)} %get-tuple-element.86, f32[4,1568]{1,0:T(4,128)S(1)} %log_add_fusion), kind=kOutput, calls=%fused_computation.44 | convolution fusion | flops 1279688448 | bytes 40969728 | tf_op jit(solution)/shard_map/hqk,qhd->khd/dot_general | solution.py:239
  845.0 26.4 %multiply_reduce_fusion = (f32[4,1568]{1,0:T(4,128)S(1)}, f32[4,1568,1568]{1,2,0:T(8,128)}) fusion(f32[4,1568,1568]{1,2,0:T(8,128)} %get-tuple-element.86, f32[4,1568]{1,0:T(4,128)S(1)} %log_add_fusion, bf16[1568,4,64]{0,2,1:T(8,128)(2,1)S(1)} %bitcast.105, f32[1568,4,64]{0,2,1:T(8,128)S(1)} %bitcast.107, f32[4,64]{1,0:T(4,128)S(1)} %copy.71), kind=kOutput, calls=%fused_computation.1 | convolution fusion | flops 1289115520 | bytes 81135616 | tf_op jit(solution)/shard_map/qhd,khd->hqk/dot_general | solution.py:226
  871.3 33.5 %multiply_convert_fusion = bf16[4,1568,1568]{1,2,0:T(8,128)(2,1)} fusion(f32[4,1568,1568]{1,2,0:T(8,128)} %get-tuple-element.90, f32[4,1568,1568]{1,2,0:T(8,128)} %get-tuple-element.86, f32[4,1568]{1,0:T(4,128)S(1)} %get-tuple-element.89, f32[4,1568]{1,0:T(4,128)S(1)} %log_add_fusion), kind=kLoop, calls=%fused_computation | loop fusion | flops 39337984 | bytes 98395136 | tf_op jit(solution)/shard_map/convert_element_type | solution.py:230
  904.9 11.4 fusion.16
  916.3 10.4 convert_reduce_fusion.3
  929.9 7.3 convolution_bitcast_fusion
  938.9 6.7 fusion.27
  945.7 103.3 %reduce-scatter.25.cloned.1.call-done = f32[392,1024]{1,0:T(8,128)} async-done(((f32[1568,1024]{1,0:T(8,128)}), f32[392,1024]{1,0:T(8,128)}) %reduce-scatter.25.cloned.1.call-update) | async-done | bytes 1605648 | tf_op jit(solution)/shard_map/reduce_scatter | solution.py:101
  1049.0 2.2 fusion.36
  1053.4 8.8 fusion.54
  1062.6 8.9 fusion.55
  1072.8 4.0 fusion.53
  1078.0 8.6 reduce-scatter.39.cloned.1.call-done
  1086.6 1.4 copy.95
  1088.1 12.2 all-reduce
  1100.9 35.8 %reduce-scatter.27.cloned.1.call-done = f32[3,128,256]{1,2,0:T(8,128)} async-done(((f32[3,1024,256]{1,2,0:T(8,128)}), f32[3,128,256]{1,2,0:T(8,128)}) %reduce-scatter.27.cloned.1.call-update) | async-done | bytes 393232 | tf_op jit(solution)/shard_map/reduce_scatter | solution.py:278
  1136.7 1.9 copy.83
  1138.6 3.1 fusion.35
  1141.7 131.2 %reduce-scatter.35.cloned.1.call-done = f32[32,2]{1,0:T(8,128)} async-done(((f32[1024,2]{1,0:T(8,128)}), f32[32,2]{1,0:T(8,128)}) %reduce-scatter.35.cloned.1.call-update) | async-done | bytes 272
  1274.3 131.3 %reduce-scatter.37.cloned.1.call-done = f32[32,4]{1,0:T(8,128)} async-done(((f32[1024,4]{1,0:T(8,128)}), f32[32,4]{1,0:T(8,128)}) %reduce-scatter.37.cloned.1.call-update) | async-done | bytes 528
  1406.9 50.1 %reduce-scatter.31.cloned.1.call-done = f32[128,1024]{1,0:T(8,128)} async-done(((f32[1024,1024]{1,0:T(8,128)}), f32[128,1024]{1,0:T(8,128)}) %reduce-scatter.31.cloned.1.call-update) | async-done | bytes 524304 | tf_op jit(solution)/shard_map/reduce_scatter | solution.py:280
  1457.0 55.5 %reduce-scatter.33.cloned.1.call-done = f32[1024,128]{1,0:T(8,128)} async-done(((f32[1024,1024]{1,0:T(8,128)}), f32[1024,128]{1,0:T(8,128)}) %reduce-scatter.33.cloned.1.call-update) | async-done | bytes 524304 | tf_op jit(solution)/shard_map/reduce_scatter | solution.py:281
  1512.5 39.6 %reduce-scatter.29.cloned.1.call-done = f32[256,128]{1,0:T(8,128)} async-done(((f32[256,1024]{1,0:T(8,128)}), f32[256,128]{1,0:T(8,128)}) %reduce-scatter.29.cloned.1.call-update) | async-done | bytes 131088 | tf_op jit(solution)/shard_map/reduce_scatter | solution.py:279
  (144 shorter events, 27.3 us)
Async XLA Ops:
  7.2 196.2 %all-gather.8.cloned.1.call-start = ((), (), s32[]{:S(2)}) async-start(), calls=%async_computation.11 | async-start | bytes 1769472 | tf_op jit(solution)/shard_map/all_gather | solution.py:44
  7.9 375.5 %reduce-scatter.19.cloned.1.call-start = ((), (), s32[]{:S(2)}) async-start(), calls=%async_computation.12 | async-start | bytes 8028160 | tf_op jit(solution)/shard_map/reduce_scatter | solution.py:88
  9.3 137.2 %copy-start.2 = (bf16[392,1024]{1,0:T(8,128)(2,1)S(1)}, bf16[392,1024]{1,0:T(8,128)(2,1)}, u32[]{:S(2)}) copy-start(bf16[392,1024]{1,0:T(8,128)(2,1)} %param.11) | copy-start | bytes 2408452
  9.3 138.5 %copy-start.21 = (f32[392]{0:T(512)}, f32[392]{0:T(512)S(1)}, u32[]{:S(2)}) copy-start(f32[392]{0:T(512)S(1)} %broadcast_multiply_fusion.5) | copy-start | bytes 4708
  144.4 3.4 copy-start.23
  144.4 3.4 copy-start.18
  144.4 35.4 %copy-start.25 = (bf16[2,4,8]{2,1,0:T(4,128)(2,1)S(1)}, bf16[2,4,8]{2,1,0:T(4,128)(2,1)}, u32[]{:S(2)}) copy-start(bf16[2,4,8]{2,1,0:T(4,128)(2,1)} %param.17) | copy-start | bytes 388
  144.4 43.8 %copy-start.20 = (bf16[256,128]{1,0:T(8,128)(2,1)S(1)}, bf16[256,128]{1,0:T(8,128)(2,1)}, u32[]{:S(2)}) copy-start(bf16[256,128]{1,0:T(8,128)(2,1)} %param.18) | copy-start | bytes 196612
  147.8 22.7 %collective-permute-start = (bf16[392,1024]{1,0:T(8,128)(2,1)S(1)}, bf16[392,1024]{1,0:T(8,128)(2,1)S(1)}, u32[]{:S(2)}, u32[]{:S(2)}) collective-permute-start(bf16[392,1024]{1,0:T(8,128)(2,1)S(1)} %get-tuple-element.73), channel_id=1, source_target_pairs={{0,1},{1,2},{2,3},{3,0},{4,5},{5,6},{6,7},{7,4},{8,9},{9,10},{10,1... | collective-permute-start | bytes 2408456 | tf_op jit(solution)/shard_map/ppermute | solution.py:73
  150.0 50.3 %collective-permute-start.1 = (bf16[392,1024]{1,0:T(8,128)(2,1)S(1)}, bf16[392,1024]{1,0:T(8,128)(2,1)S(1)}, u32[]{:S(2)}, u32[]{:S(2)}) collective-permute-start(bf16[392,1024]{1,0:T(8,128)(2,1)S(1)} %get-tuple-element.73), channel_id=1, source_target_pairs={{0,3},{1,0},{2,1},{3,2},{4,7},{5,4},{6,5},{7,6},{8,11},{9,8},{10,9... | collective-permute-start | bytes 2408456 | tf_op jit(solution)/shard_map/ppermute | solution.py:78
  170.5 30.8 %collective-permute-start.2 = (bf16[392,1024]{1,0:T(8,128)(2,1)S(1)}, bf16[392,1024]{1,0:T(8,128)(2,1)}, u32[]{:S(2)}, u32[]{:S(2)}) collective-permute-start(bf16[392,1024]{1,0:T(8,128)(2,1)S(1)} %collective-permute-done), channel_id=1, source_target_pairs={{0,1},{1,2},{2,3},{3,0},{4,5},{5,6},{6,7},{7,4},{8,9},{9,10},{10,1... | collective-permute-start | bytes 2408456 | tf_op jit(solution)/shard_map/ppermute | solution.py:73
  188.2 27.5 %copy-start.16 = (f32[4,64]{1,0:T(4,128)}, f32[4,64]{1,0:T(4,128)S(1)}, u32[]{:S(2)}) copy-start(f32[4,64]{1,0:T(4,128)S(1)} %copy.73) | copy-start | bytes 3076
  212.3 3.4 copy-start
  215.7 16.2 %copy-start.3 = (f32[1,1568,256]{1,2,0:T(8,128)}, f32[1,1568,256]{1,2,0:T(8,128)S(1)}, u32[]{:S(2)}) copy-start(f32[1,1568,256]{1,2,0:T(8,128)S(1)} %copy.72) | copy-start | bytes 4816900
  231.9 16.4 %copy-start.5 = (f32[1,1568,256]{1,2,0:T(8,128)S(1)}, f32[1,1568,256]{1,2,0:T(8,128)}, u32[]{:S(2)}) copy-start(f32[1,1568,256]{1,2,0:T(8,128)} %copy.69) | copy-start | bytes 4816900
  248.3 17.4 %copy-start.10 = (bf16[256,1024]{1,0:T(8,128)(2,1)S(1)}, bf16[256,1024]{1,0:T(8,128)(2,1)}, u32[]{:S(2)}) copy-start(bf16[256,1024]{1,0:T(8,128)(2,1)} %all_gather.42) | copy-start | bytes 1572868
  270.6 2.0 copy-start.9
  270.7 174.9 %all-gather.10.cloned.1.call-start = ((), (), s32[]{:S(2)}) async-start(), calls=%async_computation.13 | async-start | bytes 2359296 | tf_op jit(solution)/shard_map/all_gather | solution.py:46
  271.4 182.8 %all-gather.12.cloned.1.call-start = ((), (), s32[]{:S(2)}) async-start(), calls=%async_computation.14 | async-start | bytes 2359296 | tf_op jit(solution)/shard_map/all_gather | solution.py:47
  272.0 238.3 %all-gather.14.cloned.1.call-start = ((), (), s32[]{:S(2)}) async-start(), calls=%async_computation.16 | async-start | bytes 4014080 | tf_op jit(solution)/shard_map/all_gather | solution.py:97
  273.8 365.1 %reduce-scatter.23.cloned.1.call-start = ((), (), s32[]{:S(2)}) async-start(), calls=%async_computation.17 | async-start | bytes 8028160 | tf_op jit(solution)/shard_map/reduce_scatter | solution.py:101
  387.5 38.5 %copy-start.27 = (bf16[1,128]{1,0:T(2,128)(2,1)S(1)}, bf16[1,128]{1,0:T(2,128)(2,1)}, u32[]{:S(2)}) copy-start(bf16[1,128]{1,0:T(2,128)(2,1)} %param.20) | copy-start | bytes 772
  388.7 22.6 %collective-permute-start.3 = (bf16[392,1024]{1,0:T(8,128)(2,1)S(1)}, bf16[392,1024]{1,0:T(8,128)(2,1)S(1)}, u32[]{:S(2)}, u32[]{:S(2)}) collective-permute-start(bf16[392,1024]{1,0:T(8,128)(2,1)S(1)} %get-tuple-element.69), channel_id=1, source_target_pairs={{0,1},{1,2},{2,3},{3,0},{4,5},{5,6},{6,7},{7,4},{8,9},{9,10},{10,1... | collective-permute-start | bytes 2408456 | tf_op jit(solution)/shard_map/ppermute | solution.py:73
  390.3 45.4 %collective-permute-start.4 = (bf16[392,1024]{1,0:T(8,128)(2,1)S(1)}, bf16[392,1024]{1,0:T(8,128)(2,1)S(1)}, u32[]{:S(2)}, u32[]{:S(2)}) collective-permute-start(bf16[392,1024]{1,0:T(8,128)(2,1)S(1)} %get-tuple-element.69), channel_id=1, source_target_pairs={{0,3},{1,0},{2,1},{3,2},{4,7},{5,4},{6,5},{7,6},{8,11},{9,8},{10,9... | collective-permute-start | bytes 2408456 | tf_op jit(solution)/shard_map/ppermute | solution.py:78
  411.4 33.3 %collective-permute-start.5 = (bf16[392,1024]{1,0:T(8,128)(2,1)S(1)}, bf16[392,1024]{1,0:T(8,128)(2,1)S(1)}, u32[]{:S(2)}, u32[]{:S(2)}) collective-permute-start(bf16[392,1024]{1,0:T(8,128)(2,1)S(1)} %collective-permute-done.3), channel_id=1, source_target_pairs={{0,1},{1,2},{2,3},{3,0},{4,5},{5,6},{6,7},{7,4},{8,9},{9,10},{10,1... | collective-permute-start | bytes 2408456 | tf_op jit(solution)/shard_map/ppermute | solution.py:73
  510.3 11.2 copy-start.28
  519.8 1.7 copy-start.30
  527.2 227.4 %reduce-scatter.21.cloned.1.call-start = ((), (), s32[]{:S(2)}) async-start(), calls=%async_computation.15 | async-start | bytes 8028160 | tf_op jit(solution)/shard_map/reduce_scatter | solution.py:88
  536.1 288.3 %all-gather.16.cloned.1.call-start = ((), (), s32[]{:S(2)}) async-start(), calls=%async_computation.18 | async-start | bytes 4014080 | tf_op jit(solution)/shard_map/all_gather | solution.py:97
  759.1 289.9 %reduce-scatter.25.cloned.1.call-start = ((), (), s32[]{:S(2)}) async-start(), calls=%async_computation.19 | async-start | bytes 8028160 | tf_op jit(solution)/shard_map/reduce_scatter | solution.py:101
  828.0 16.9 %copy-start.6 = (f32[1,1568,256]{1,2,0:T(8,128)S(1)}, f32[1,1568,256]{1,2,0:T(8,128)}, u32[]{:S(2)}) copy-start(f32[1,1568,256]{1,2,0:T(8,128)} %copy.69) | copy-start | bytes 4816900
  871.3 33.5 %copy-start.4 = (f32[1,1568,256]{1,2,0:T(8,128)S(1)}, f32[1,1568,256]{1,2,0:T(8,128)}, u32[]{:S(2)}) copy-start(f32[1,1568,256]{1,2,0:T(8,128)} %copy-done.3) | copy-start | bytes 4816900
  871.3 33.5 %copy-start.17 = (f32[4,64]{1,0:T(4,128)S(1)}, f32[4,64]{1,0:T(4,128)}, u32[]{:S(2)}) copy-start(f32[4,64]{1,0:T(4,128)} %copy-done.16) | copy-start | bytes 3076
  904.9 11.4 copy-start.1
  916.3 10.4 copy-start.8
  927.9 2.0 copy-start.12
  929.9 7.4 copy-start.14
  937.3 1.2 copy-start.13
  937.3 1.6 copy-start.15
  937.3 149.3 %reduce-scatter.39.cloned.1.call-start = ((), (), s32[]{:S(2)}) async-start(), calls=%async_computation.26 | async-start | bytes 589824
  938.4 198.2 %reduce-scatter.27.cloned.1.call-start = ((), (), s32[]{:S(2)}) async-start(), calls=%async_computation.20 | async-start | bytes 3538944 | tf_op jit(solution)/shard_map/reduce_scatter | solution.py:278
  945.6 103.4 %copy-start.19 = (f32[1,1024]{1,0:T(1,128)S(1)}, f32[1,1024]{1,0:T(1,128)}, u32[]{:S(2)}) copy-start(f32[1,1024]{1,0:T(1,128)} %copy-done.18) | copy-start | bytes 12292
  945.6 103.4 %copy-start.22 = (f32[392]{0:T(512)S(1)}, f32[392]{0:T(512)}, u32[]{:S(2)}) copy-start(f32[392]{0:T(512)} %copy-done.21) | copy-start | bytes 4708
  945.6 103.4 %copy-start.24 = (f32[392]{0:T(512)S(1)}, f32[392]{0:T(512)}, u32[]{:S(2)}) copy-start(f32[392]{0:T(512)} %copy-done.23) | copy-start | bytes 4708
  945.6 327.3 %reduce-scatter.35.cloned.1.call-start = ((), (), s32[]{:S(2)}) async-start(), calls=%async_computation.24 | async-start | bytes 540672
  1052.3 353.3 %reduce-scatter.37.cloned.1.call-start = ((), (), s32[]{:S(2)}) async-start(), calls=%async_computation.25 | async-start | bytes 540672
  1053.4 403.6 %reduce-scatter.31.cloned.1.call-start = ((), (), s32[]{:S(2)}) async-start(), calls=%async_computation.22 | async-start | bytes 4718592 | tf_op jit(solution)/shard_map/reduce_scatter | solution.py:280
  1062.3 450.2 %reduce-scatter.33.cloned.1.call-start = ((), (), s32[]{:S(2)}) async-start(), calls=%async_computation.23 | async-start | bytes 4718592 | tf_op jit(solution)/shard_map/reduce_scatter | solution.py:281
  1071.6 1.2 copy-start.11
  1071.6 5.2 copy-start.29
  1071.6 480.6 %reduce-scatter.29.cloned.1.call-start = ((), (), s32[]{:S(2)}) async-start(), calls=%async_computation.21 | async-start | bytes 1179648 | tf_op jit(solution)/shard_map/reduce_scatter | solution.py:279
  1076.8 61.8 %copy-start.7 = (f32[392,1024]{1,0:T(8,128)S(1)}, f32[392,1024]{1,0:T(8,128)}, u32[]{:S(2)}) copy-start(f32[392,1024]{1,0:T(8,128)} %reduce-scatter.25.cloned.1.call-done) | copy-start | bytes 4816900
  1406.4 145.8 %copy-start.26 = (f32[4,32]{1,0:T(4,128)}, f32[4,32]{1,0:T(4,128)S(1)}, u32[]{:S(2)}) copy-start(f32[4,32]{1,0:T(4,128)S(1)} %copy.91) | copy-start | bytes 1540
Sparse Core Ops, SparseCore 0:
  9.9 28.3 all-gather.7
  270.8 112.5 reduce-scatter.18
  385.3 28.4 all-gather.9
  415.4 28.1 all-gather.11
  445.7 64.5 all-gather.13
  527.3 111.5 reduce-scatter.22
  641.2 113.3 reduce-scatter.20
  759.2 65.0 all-gather.15
  937.4 111.5 reduce-scatter.24
  1051.9 34.6 reduce-scatter.38
  1090.4 46.2 reduce-scatter.26
  1138.8 134.0 reduce-scatter.34
  1275.2 130.3 reduce-scatter.36
  1409.4 47.6 reduce-scatter.30
  1461.2 51.3 reduce-scatter.32
  1516.1 35.9 reduce-scatter.28
